TPU v7x, 256 devices: a whole 4x4x8 slice. The times are simulated.
256 devices in a mesh: layer: 4 (over z_hi, core), doc: 64 (over y, x, z_lo).
Axes of the slice: x: 4, y: 4, z: 8 (z_hi: 2, z_lo: 4; z = z_hi * 4 + z_lo), core: 2. Of those that a mesh axis runs over, the one named last changes fastest.
Arguments:
- query_grads: bfloat16 [4, 256, 4096], P('layer', 'doc'), may hold values from -6 to 6
- stored_grads: bfloat16 [4, 65536, 4096], P('layer', 'doc'), may hold values from -0.0234375 to 0.0234375
- basis_in: float32 [4, 64, 64], P('layer'), may hold values from -0.75 to 0.75
- basis_out: float32 [4, 64, 64], P('layer'), may hold values from -0.75 to 0.75
- eigen_values: float32 [4, 64, 64], P('layer'), may hold values from 0.02 to 4
- layer_mask: int32 [256, 4], P(None, 'layer'), may hold values 0 or 1
- doc_counts: int32 [64], P('doc'), may hold values from 1 to 1024, 32768 in all
Outputs:
- scores: float32 [256, 65536], P('layer', 'doc')
Inputs may be any that keep to these rules, and one draw needn't show every extreme that they name: `doc_counts`: the counts sum to 32768 and the largest equals 1024.
All inputs are finite; a program needn't handle non-finite values. No bound on the sum of `layer_mask` or of `doc_counts` on one device may be relied on, other than what follows from the above.
Results may differ from a plain program's by a relative error of at most 0.0029.
Values may be sent and summed in bfloat16 or wider, within the bound.
No kernel may reach another device: no remote copies, remote signals or barrier semaphores. Data moves between devices by JAX's collectives and lax.ppermute only.
A program may use at most 64 MiB of HBM per device.

v0:
```python
import jax
import jax.numpy as jnp
from jax import lax
from jax.sharding import PartitionSpec as P

damping = 0.1


def precondition(gradients, basis_in, basis_out, eigen_values):
    row_count = gradients.shape[0]
    grid_blocks = gradients.astype(jnp.float32).reshape(
        row_count, basis_out.shape[0], basis_in.shape[0]
    )
    rotated = jnp.einsum(
        "xi,qxy,yj->qij", basis_out, grid_blocks, basis_in, precision=lax.Precision.HIGHEST
    )
    scaled = rotated / (eigen_values + damping)
    restored = jnp.einsum(
        "bi,qij,aj->qba", basis_out, scaled, basis_in, precision=lax.Precision.HIGHEST
    )
    return restored.reshape(row_count, -1).astype(jnp.bfloat16)


def on_device(query_grads, stored_grads, basis_in, basis_out, eigen_values, layer_mask, doc_counts):
    stored = stored_grads[0]
    base_in = basis_in[0]
    base_out = basis_out[0]
    eigens = eigen_values[0]
    row_weights = layer_mask[:, 0].astype(jnp.bfloat16)
    own_rows = precondition(query_grads[0], base_in, base_out, eigens)
    masked = lax.all_gather(own_rows, "doc", axis=0, tiled=True) * row_weights[:, None]
    score_tiles = lax.dot_general(
        masked, stored, (((1,), (1,)), ((), ())), preferred_element_type=jnp.float32
    )
    live_slots = jnp.arange(stored.shape[0], dtype=jnp.int32) < doc_counts[0]
    score_tiles = jnp.where(live_slots[None, :], score_tiles, jnp.zeros_like(score_tiles))
    return lax.psum_scatter(score_tiles, "layer", scatter_dimension=0, tiled=True)


def solution(mesh):
    in_specs = (
        P("layer", "doc", None),
        P("layer", "doc", None),
        P("layer", None, None),
        P("layer", None, None),
        P("layer", None, None),
        P(None, "layer"),
        P("doc"),
    )
    out_specs = P("layer", "doc")
    return jax.shard_map(
        on_device, mesh=mesh, in_specs=in_specs, out_specs=out_specs, check_vma=False
    )
```

profile of v0, /device:TPU:1, one launch (start us, length us, event | category | flops | bytes accessed | tf_op | source)
XLA Modules:
  0.0 424.5 jit_solution(11922888940631086043)
XLA Ops:
  6.5 0.0 copy-start
  6.5 0.0 all-gather.3.cloned.1.call-start
  6.5 0.9 reshape.10
  7.4 0.8 add_bitcast_fusion
  8.2 0.0 copy-done
  8.2 0.3 fusion.13
  8.5 1.1 convolution_divide_fusion
  9.6 0.3 fusion.11
  9.9 1.0 convolution_convert_fusion
  10.9 0.7 reshape.11
  11.6 0.0 all-gather.3.cloned.1.call-update
  11.7 0.0 reduce-scatter.2.cloned.1.call-start
  12.4 0.7 convert_reduce_fusion
  13.1 306.5 %all-gather.3.cloned.1.call-done = bf16[64,4,4096]{2,1,0:T(4,128)(2,1)} async-done(((bf16[1,4,4096]{2,1,0:T(4,128)(2,1)}), bf16[64,4,4096]{2,1,0:T(4,128)(2,1)}) %all-gather.3.cloned.1.call-update) | async-done | bytes 2097168 | tf_op jit(solution)/shard_map/all_gather | solution.py:31
  319.6 2.5 reshape.12
  322.1 6.7 %fusion.3 = f32[256,1024]{1,0:T(8,128)} fusion(bf16[1,1024,4096]{2,1,0:T(8,128)(2,1)} %param.8, bf16[256,4096]{1,0:T(8,128)(2,1)S(1)} %reshape.12, bf16[256]{0:T(256)(128)(2,1)S(1)} %convert_reduce_fusion, pred[1024]{0:T(1024)(128)(4,1)S(1)} %iota_compare_fusion), kind=kOutput, calls=%fused_computation.3 | convolution fusion | flops 2148794368 | bytes 11535872 | tf_op jit(solution)/shard_map/dot_general | solution.py:32
  328.9 0.0 reduce-scatter.2.cloned.1.call-update
  328.9 88.8 %reduce-scatter.2.cloned.1.call-done = f32[64,1024]{1,0:T(8,128)} async-done(((f32[256,1024]{1,0:T(8,128)}), f32[64,1024]{1,0:T(8,128)}) %reduce-scatter.2.cloned.1.call-update) | async-done | bytes 262160 | tf_op jit(solution)/shard_map/reduce_scatter | solution.py:37
  (1 shorter events, 0.0 us)
Async XLA Ops:
  6.5 1.7 copy-start
  6.5 313.1 %all-gather.3.cloned.1.call-start = ((), (), s32[]{:S(2)}) async-start(), calls=%async_computation.2 | async-start | bytes 2129920 | tf_op jit(solution)/shard_map/all_gather | solution.py:31
  11.7 406.0 %reduce-scatter.2.cloned.1.call-start = ((), (), s32[]{:S(2)}) async-start(), calls=%async_computation.1 | async-start | bytes 1310720 | tf_op jit(solution)/shard_map/reduce_scatter | solution.py:37
Sparse Core Ops, SparseCore 0:
  11.8 307.7 all-gather.2
  329.0 88.6 reduce-scatter.1
where the time goes:
time: 425 us
  waiting for transfers between devices  395 us (93%)
  between operations  14.1 us (3%)
  matrix products  9.42 us (2%)
    all_gather x1, waiting for transfers between devices, on_device(): lax.all_gather(own_rows, 'doc', axis=0, tiled=True) * row_weights[:, None]  307 us
    reduce_scatter x1, waiting for transfers between devices, on_device(): lax.psum_scatter(score_tiles, 'layer', scatter_dimension=0, tiled=True)  88.8 us
  transfers between devices with their start and end apart: 2, of which 2 were waited for; matrix products, arithmetic and copies ran while one was open for 0% of the time, Pallas kernels for 0%

commit v1 on v0

--- a/solution.py
+++ b/solution.py
@@ -28,7 +28,12 @@
     eigens = eigen_values[0]
     row_weights = layer_mask[:, 0].astype(jnp.bfloat16)
     own_rows = precondition(query_grads[0], base_in, base_out, eigens)
-    masked = lax.all_gather(own_rows, "doc", axis=0, tiled=True) * row_weights[:, None]
+    masked = (
+        jnp.concatenate(
+            lax.all_to_all(jnp.stack([own_rows] * lax.axis_size("doc")), "doc", 0, 0), axis=0
+        )
+        * row_weights[:, None]
+    )
     score_tiles = lax.dot_general(
         masked, stored, (((1,), (1,)), ((), ())), preferred_element_type=jnp.float32
     )

time: 425 us -> 138 us (0.32)
  waiting for transfers between devices: 395 us -> 92.4 us
  starting transfers between devices: 0.04 us -> 12.7 us
    all_gather x1 -> x0, waiting for transfers between devices: 307 us -> none  [on_device(): lax.all_gather(own_rows, 'doc', axis=0, tiled=True) * row_weights[:, None]]
    all_to_all x0 -> x1, waiting for transfers between devices: none -> 49.5 us  [on_device(): lax.all_to_all(jnp.stack([own_rows] * lax.axis_size('doc')), 'doc', 0, 0)]
    reduce_scatter x1, waiting for transfers between devices: 88.8 us -> 42.9 us  [on_device(): lax.psum_scatter(score_tiles, 'layer', scatter_dimension=0, tiled=True)]
    all_to_all x0 -> x1, starting transfers between devices: none -> 12.7 us  [on_device(): lax.all_to_all(jnp.stack([own_rows] * lax.axis_size('doc')), 'doc', 0, 0)]
where the time goes in v1:
time: 138 us
  waiting for transfers between devices  92.4 us (67%)
  between operations  14.1 us (10%)
  starting transfers between devices  12.7 us (9%)
  matrix products  9.41 us (7%)
  local copies, waits for them, and re-layouts  6.01 us (4%)
  other arithmetic  3.12 us (2%)
    all_to_all x1, waiting for transfers between devices, on_device(): lax.all_to_all(jnp.stack([own_rows] * lax.axis_size('doc')), 'doc', 0, 0)  49.5 us
    reduce_scatter x1, waiting for transfers between devices, on_device(): lax.psum_scatter(score_tiles, 'layer', scatter_dimension=0, tiled=True)  42.9 us
    all_to_all x1, starting transfers between devices, on_device(): lax.all_to_all(jnp.stack([own_rows] * lax.axis_size('doc')), 'doc', 0, 0)  12.7 us
    dot_general x1, matrix products, on_device(): lax.dot_general(masked, stored, (((1,), (1,)), ((), ())), preferred_eleme...  6.72 us
  transfers between devices with their start and end apart: 2, of which 2 were waited for; matrix products, arithmetic and copies ran while one was open for 0% of the time, Pallas kernels for 0%

profile of v1, /device:TPU:1, one launch (start us, length us, event | category | flops | bytes accessed | tf_op | source)
XLA Modules:
  0.0 137.8 jit_solution(9609637693861954365)
XLA Ops:
  6.5 0.0 copy-start
  6.5 0.9 reshape.20
  7.4 0.8 add_bitcast_fusion
  8.2 0.0 copy-done
  8.2 0.3 fusion.9
  8.5 1.1 convolution_divide_fusion
  9.6 0.3 fusion.7
  9.9 1.0 convolution_convert_fusion
  10.9 0.1 convert_element_type.14
  11.0 2.4 %stack.2 = bf16[64,4,4096]{2,1,0:T(4,128)(2,1)} broadcast(bf16[4,4096]{1,0:T(4,128)(2,1)S(1)} %convert_element_type.14), dimensions={1,2} | broadcast | bytes 2129920 | tf_op jit(solution)/shard_map/stack | solution.py:33
  13.4 0.0 copy-start.1
  13.4 12.7 %all-to-all-start = ((bf16[64,4,4096]{2,1,0:T(4,128)(2,1)}), bf16[64,4,4096]{2,1,0:T(4,128)(2,1)S(1)}, u32[]{:S(2)}, u32[]{:S(2)}) async-start(bf16[64,4,4096]{2,1,0:T(4,128)(2,1)} %stack.2), calls=%async_computation | async-start | bytes 4194304 | tf_op jit(solution)/shard_map/all_to_all | solution.py:33
  26.1 0.0 reduce-scatter.2.cloned.1.call-start
  26.1 0.0 copy-done.1
  26.1 0.1 mul.13
  26.9 49.5 %all-to-all-done = bf16[64,4,4096]{2,1,0:T(4,128)(2,1)S(1)} async-done(((bf16[64,4,4096]{2,1,0:T(4,128)(2,1)}), bf16[64,4,4096]{2,1,0:T(4,128)(2,1)S(1)}, u32[]{:S(2)}, u32[]{:S(2)}) %all-to-all-start) | async-done | bytes 2097184 | tf_op jit(solution)/shard_map/all_to_all | solution.py:33
  76.4 2.3 %broadcast_multiply_fusion = bf16[64,4,4096]{2,1,0:T(4,128)(2,1)} fusion(bf16[64,4,4096]{2,1,0:T(4,128)(2,1)S(1)} %all-to-all-done, bf16[64,4]{1,0:T(8,128)(2,1)S(1)} %mul.13), kind=kLoop, calls=%fused_computation.5 | loop fusion | flops 1048576 | bytes 4194816 | tf_op jit(solution)/shard_map/mul | solution.py:32
  78.8 2.5 %mul.16 = bf16[256,4096]{1,0:T(8,128)(2,1)S(1)} reshape(bf16[64,4,4096]{2,1,0:T(4,128)(2,1)} %broadcast_multiply_fusion) | data formatting | bytes 4194304 | tf_op jit(solution)/shard_map/mul | solution.py:32
  81.3 6.7 %fusion.2 = f32[256,1024]{1,0:T(8,128)} fusion(bf16[256,4096]{1,0:T(8,128)(2,1)S(1)} %mul.16, bf16[1,1024,4096]{2,1,0:T(8,128)(2,1)} %param.8, pred[1024]{0:T(1024)(128)(4,1)S(1)} %iota_compare_fusion), kind=kOutput, calls=%fused_computation.2 | convolution fusion | flops 2147745792 | bytes 11535360 | tf_op jit(solution)/shard_map/dot_general | solution.py:37
  88.0 0.0 reduce-scatter.2.cloned.1.call-update
  88.1 42.9 %reduce-scatter.2.cloned.1.call-done = f32[64,1024]{1,0:T(8,128)} async-done(((f32[256,1024]{1,0:T(8,128)}), f32[64,1024]{1,0:T(8,128)}) %reduce-scatter.2.cloned.1.call-update) | async-done | bytes 262160 | tf_op jit(solution)/shard_map/reduce_scatter | solution.py:42
  (2 shorter events, 0.0 us)
Async XLA Ops:
  6.5 1.7 %copy-start = (f32[1,64,64]{2,1,0:T(8,128)S(1)}, f32[1,64,64]{2,1,0:T(8,128)}, u32[]{:S(2)}) copy-start(f32[1,64,64]{2,1,0:T(8,128)} %param.10) | copy-start | bytes 49156
  13.4 12.7 %copy-start.1 = (s32[256,1]{0,1:T(1,128)S(1)}, s32[256,1]{0,1:T(1,128)}, u32[]{:S(2)}) copy-start(s32[256,1]{0,1:T(1,128)} %param.12) | copy-start | bytes 3076
  13.4 63.1 %all-to-all-start = ((bf16[64,4,4096]{2,1,0:T(4,128)(2,1)}), bf16[64,4,4096]{2,1,0:T(4,128)(2,1)S(1)}, u32[]{:S(2)}, u32[]{:S(2)}) async-start(bf16[64,4,4096]{2,1,0:T(4,128)(2,1)} %stack.2), calls=%async_computation | async-start | bytes 4194304 | tf_op jit(solution)/shard_map/all_to_all | solution.py:33
  26.1 104.9 %reduce-scatter.2.cloned.1.call-start = ((), (), s32[]{:S(2)}) async-start(), calls=%async_computation.2 | async-start | bytes 1310720 | tf_op jit(solution)/shard_map/reduce_scatter | solution.py:42
Sparse Core Ops, SparseCore 0:
  88.2 42.7 reduce-scatter.1
